TPU v7x, 32 devices: a whole 2x2x4 slice. The times are simulated.
32 devices in a mesh: regions: 2 (over y), gz: 8 (over z, x), gy: 2 (over core).
Axes of the slice: x: 2, y: 2, z: 4, core: 2. Of those that a mesh axis runs over, the one named last changes fastest.
Arguments:
- iterate: float32 [16, 32, 128, 256], P(None, ('regions', 'gz'), 'gy'), parts along dimension 1, may hold values from -6 to 6
- residual: float32 [16, 32, 128, 256], P(None, ('regions', 'gz'), 'gy'), parts along dimension 1, may hold values from -16 to 16
- labels: int32 [32, 128, 256], P(('regions', 'gz'), 'gy'), parts along dimension 0, may hold values from 0 to 7
- boundary: int32 [32, 128, 256], P(('regions', 'gz'), 'gy'), parts along dimension 0, may hold values 0 or 1
Outputs:
- iterate_out: float32 [16, 32, 128, 256], P(None, ('regions', 'gz'), 'gy'), parts along dimension 1
- residual_out: float32 [16, 32, 128, 256], P(None, ('regions', 'gz'), 'gy'), parts along dimension 1
There are 2 independent parts, one for each index of `regions`. A program takes and returns all parts, laid end to end along the dimension named above; each array names one. Nothing has to cross between parts.
All inputs are finite; a program needn't handle non-finite values. No bound on the sum of `boundary` on one device may be relied on, other than what follows from the above.
Results may differ from a plain program's by a relative error of at most 0.0003.
Values sent between devices are 32-bit elements; how exact they have to be, the bound alone decides.
A program may use at most 128 MiB of HBM per device.

v0:
```python
import math
import jax
import jax.numpy as jnp
from jax import lax
from jax.sharding import PartitionSpec as P

NCLASS = 8
ITERS = 3
contrast_log = 4.0 * math.log(10.0)
highest = lax.Precision.HIGHEST


def extended_2(cells, sides, width):
    for axis, dim in sides:
        count = lax.axis_size(axis)
        ends = count - 1
        head = lax.slice_in_dim(cells, 0, width, axis=dim)
        tail = lax.slice_in_dim(cells, cells.shape[dim] - width, cells.shape[dim], axis=dim)
        cells = jnp.concatenate(
            [
                lax.ppermute(tail, axis, [(i, (i + 1) % count) for i in range(ends)]),
                cells,
                lax.ppermute(head, axis, [((i + 1) % count, i) for i in range(ends)]),
            ],
            axis=dim,
        )
    return cells


def shift_cells(block, forward):
    widths = [(0, 0)] * (block.ndim - 1)
    if forward:
        return jnp.pad(block[..., 1:], widths + [(0, 1)])
    return jnp.pad(block[..., :-1], widths + [(1, 0)])


def neighbors(extended):
    center = extended[..., 1:-1, 1:-1, :]
    beside = [
        extended[..., 2:, 1:-1, :],
        extended[..., :-2, 1:-1, :],
        extended[..., 1:-1, 2:, :],
        extended[..., 1:-1, :-2, :],
        shift_cells(center, True),
        shift_cells(center, False),
    ]
    return (center, beside)


def couplings_of(extended):
    coef_center, coef_beside = neighbors(extended[0])
    inner_center, inner_beside = neighbors(extended[1])
    diagonal = jnp.zeros_like(coef_center)
    offsets = []
    for neighbor_coef, neighbor_inner in zip(coef_beside, inner_beside):
        face_coef = jnp.where(
            neighbor_coef > 0.0,
            2.0 * coef_center * neighbor_coef / (coef_center + neighbor_coef),
            coef_center,
        )
        diagonal = diagonal + face_coef
        offsets.append(inner_center * face_coef * neighbor_inner)
    diagonal = inner_center * diagonal + (1.0 - inner_center)
    return (diagonal, offsets)


def apply_operator(diagonal, offsets, extended):
    center, beside = neighbors(extended)
    coupled = offsets[0] * beside[0]
    for weight, values in zip(offsets[1:], beside[1:]):
        coupled = coupled + weight * values
    return diagonal * center - coupled


def cell_fields(labels, boundary):
    coef = jnp.exp(labels.astype(jnp.float32) * (contrast_log / (NCLASS - 1)))
    interior = (1 - boundary).astype(jnp.float32)
    return jnp.stack([coef, interior])


def gram(left_block, right_block):
    left_flat = left_block.reshape(left_block.shape[0], -1)
    right_flat = right_block.reshape(right_block.shape[0], -1)
    return lax.dot_general(left_flat, right_flat, (((1,), (1,)), ((), ())), precision=highest)


def combine(block, weights):
    flat = block.reshape(block.shape[0], -1)
    mixed = lax.dot_general(weights, flat, (((0,), (0,)), ((), ())), precision=highest)
    return mixed.reshape(block.shape)


def spd_solve(matrix, right):
    factor = jnp.linalg.cholesky(matrix)
    return jax.scipy.linalg.cho_solve((factor, True), right)


def direction_cells(field):
    return extended_2(field, (("gz", 1), ("gy", 2)), 1)


def on_device(iterate, residual, labels, boundary):
    fields = cell_fields(labels, boundary)
    extended = extended_2(fields, (("gz", 1), ("gy", 2)), 1)
    diagonal, offsets = couplings_of(extended)
    inverse_diag = 1.0 / diagonal
    scaled = inverse_diag * residual
    direction = scaled
    for iteration in range(ITERS):
        direction_ext = direction_cells(direction)
        image = apply_operator(diagonal, offsets, direction_ext)
        weighted = inverse_diag * image
        summed_rho, curvature, cross_gram, image_gram = lax.psum(
            (
                gram(residual, scaled),
                gram(direction, image),
                gram(scaled, image),
                gram(image, weighted),
            ),
            ("gz", "gy"),
        )
        step_size = spd_solve(curvature, summed_rho)
        iterate = iterate + combine(direction, step_size)
        residual = residual - combine(image, step_size)
        if iteration + 1 < ITERS:
            scaled = inverse_diag * residual
            moved = jnp.dot(cross_gram, step_size, precision=highest)
            quadratic = jnp.dot(
                step_size.T, jnp.dot(image_gram, step_size, precision=highest), precision=highest
            )
            next_rho = summed_rho - moved - moved.T + quadratic
            momentum = spd_solve(summed_rho, next_rho)
            direction = scaled + combine(direction, momentum)
            summed_rho = next_rho
    return (iterate, residual)


def solution(mesh):
    placed = (
        P(None, ("regions", "gz"), "gy", None),
        P(None, ("regions", "gz"), "gy", None),
        P(("regions", "gz"), "gy", None),
        P(("regions", "gz"), "gy", None),
    )
    return jax.shard_map(
        on_device,
        mesh=mesh,
        in_specs=placed,
        out_specs=(P(None, ("regions", "gz"), "gy", None), P(None, ("regions", "gz"), "gy", None)),
        check_vma=False,
    )
```

profile of v0, /device:TPU:0, one launch (start us, length us, event | category | flops | bytes accessed | tf_op | source)
XLA Modules:
  0.0 462.8 jit_solution(4175048000201397154)
XLA Ops:
  3.8 5.5 %collective-permute-start = (f32[2,1,64,256]{3,2,1,0:T(8,128)S(1)}, f32[2,1,64,256]{3,2,1,0:T(8,128)S(1)}, u32[]{:S(2)}, u32[]{:S(2)}) collective-permute-start(f32[2,1,64,256]{3,2,1,0:T(8,128)S(1)} %get-tuple-element.51), channel_id=1, source_target_pairs={{0,2},{2,4},{4,6},{6,8},{8,10},{10,12},{12,14},{1,3},{3,5},{5,7},{... | collective-permute-start | bytes 393224 | tf_op jit(solution)/shard_map/ppermute | solution.py:21
  9.3 1.5 collective-permute-done.1
  10.9 3.0 collective-permute-done
  15.2 3.0 collective-permute-start.2
  23.4 5.1 %collective-permute-start.5 = (f32[16,1,64,256]{3,0,2,1:T(8,128)S(1)}, f32[16,1,64,256]{3,0,2,1:T(8,128)S(1)}, u32[]{:S(2)}, u32[]{:S(2)}) collective-permute-start(f32[16,1,64,256]{3,0,2,1:T(8,128)S(1)} %get-tuple-element.35), channel_id=1, source_target_pairs={{0,2},{2,4},{4,6},{6,8},{8,10},{10,12},{12,14},{1,3},{3,5},{5,7},{... | collective-permute-start | bytes 3145736 | tf_op jit(solution)/shard_map/ppermute | solution.py:21
  28.5 3.5 fusion.74
  32.7 17.4 %collective-permute-done.4 = f32[16,1,64,256]{3,0,2,1:T(8,128)S(1)} collective-permute-done((f32[16,1,64,256]{3,0,2,1:T(8,128)S(1)}, f32[16,1,64,256]{3,0,2,1:T(8,128)S(1)}, u32[]{:S(2)}, u32[]{:S(2)}) %collective-permute-start.4) | collective-permute-done | bytes 1048608 | tf_op jit(solution)/shard_map/ppermute | solution.py:23
  50.1 22.6 %collective-permute-done.5 = f32[16,1,64,256]{3,0,2,1:T(8,128)S(1)} collective-permute-done((f32[16,1,64,256]{3,0,2,1:T(8,128)S(1)}, f32[16,1,64,256]{3,0,2,1:T(8,128)S(1)}, u32[]{:S(2)}, u32[]{:S(2)}) %collective-permute-start.5) | collective-permute-done | bytes 1048608 | tf_op jit(solution)/shard_map/ppermute | solution.py:21
  72.8 1.9 collective-permute-start.7
  74.7 1.5 collective-permute-start.6
  76.4 2.5 copy.93
  79.0 3.2 fusion.34
  82.2 3.8 convolution_bitcast_fusion.5
  86.0 2.7 fusion.86
  88.8 2.6 copy.95
  91.3 60.9 %all-reduce.12 = (f32[16,16]{0,1:T(8,128)S(1)}, f32[16,16]{0,1:T(8,128)S(1)}, f32[16,16]{1,0:T(8,128)S(1)}) all-reduce(f32[16,16]{0,1:T(8,128)S(1)} %fusion.74, f32[16,16]{0,1:T(8,128)S(1)} %convolution_bitcast_fusion.5, f32[16,16]{1,0:T(8,128)S(1)} %fusion.86), channel_id=1, replica_groups=mesh['regions'=2,'gz'=8,'gy'=2] {'gz','gy'}, use_global_device_ids=true, to_apply=%region_3.5 | all-reduce | flops 768 | bytes 6144 | tf_op jit(solution)/shard_map/psum | solution.py:113
  157.0 6.3 %copy_subtract_fusion = f32[16,2,64,256]{3,0,2,1:T(8,128)S(1)} fusion(f32[16,2,64,256]{3,2,1,0:T(8,128)} %param.8, f32[2,64,256,16]{2,1,0,3:T(8,128)} %bitcast.241, f32[16,16]{1,0:T(8,128)S(1)} %fusion.124), kind=kOutput, calls=%fused_computation.85 | convolution fusion | flops 101187584 | bytes 6292480 | tf_op jit(solution)/shard_map/dot_general | solution.py:89
  168.1 4.5 multiply_add_fusion.1
  174.1 4.6 collective-permute-start.9
  179.5 15.8 %collective-permute-done.8 = f32[16,1,64,256]{3,0,2,1:T(8,128)S(1)} collective-permute-done((f32[16,1,64,256]{3,0,2,1:T(8,128)S(1)}, f32[16,1,64,256]{3,0,2,1:T(8,128)S(1)}, u32[]{:S(2)}, u32[]{:S(2)}) %collective-permute-start.8) | collective-permute-done | bytes 1048608 | tf_op jit(solution)/shard_map/ppermute | solution.py:23
  195.3 18.0 %collective-permute-done.9 = f32[16,1,64,256]{3,0,2,1:T(8,128)S(1)} collective-permute-done((f32[16,1,64,256]{3,0,2,1:T(8,128)S(1)}, f32[16,1,64,256]{3,0,2,1:T(8,128)S(1)}, u32[]{:S(2)}, u32[]{:S(2)}) %collective-permute-start.9) | collective-permute-done | bytes 1048608 | tf_op jit(solution)/shard_map/ppermute | solution.py:21
  213.2 1.9 collective-permute-start.11
  215.2 1.8 collective-permute-start.10
  216.9 2.8 fusion.77
  219.7 2.6 copy.97
  222.3 3.2 fusion.24
  225.5 2.9 convolution_bitcast_fusion.3
  228.4 2.8 fusion.89
  231.2 2.8 fusion.80
  234.0 2.6 copy.99
  236.6 62.6 %all-reduce.11 = (f32[16,16]{0,1:T(8,128)S(1)}, f32[16,16]{0,1:T(8,128)S(1)}, f32[16,16]{1,0:T(8,128)S(1)}, f32[16,16]{1,0:T(8,128)S(1)}) all-reduce(f32[16,16]{0,1:T(8,128)S(1)} %fusion.77, f32[16,16]{0,1:T(8,128)S(1)} %convolution_bitcast_fusion.3, f32[16,16]{1,0:T(8,128)S(1)} %fusion.89, ...), channel_id=1, replica_groups=mesh['regions'=2,'gz'=8,'gy'=2] {'gz','gy'}, use_global_device_ids=true, to_apply=%region_6.9 | all-reduce | flops 1024 | bytes 8192 | tf_op jit(solution)/shard_map/psum | solution.py:113
  303.5 5.7 %fusion.68 = f32[16,2,64,256]{3,0,2,1:T(8,128)} fusion(f32[16,2,64,256]{3,0,2,1:T(8,128)S(1)} %copy_subtract_fusion, f32[2,64,256,16]{2,1,0,3:T(8,128)} %bitcast.240, f32[16,16]{1,0:T(8,128)S(1)} %fusion.113), kind=kOutput, calls=%fused_computation.89 | convolution fusion | flops 101187584 | bytes 6292480 | tf_op jit(solution)/shard_map/dot_general | solution.py:89
  314.1 5.2 %multiply_add_fusion = f32[16,2,64,256]{3,0,2,1:T(8,128)S(1)} fusion(f32[16,2,64,256]{3,0,2,1:T(8,128)} %fusion.68, f32[16,16,1,1]{0,1,3,2:T(8,128)S(1)} %convolution_bitcast_fusion.2, f32[2,64,256,16]{2,1,0,3:T(8,128)} %bitcast.234, f32[2,64,256]{2,1,0:T(8,128)S(1)} %get-tuple-element.17), kind=kOutput, calls=%fused_computation.6 | convolution fusion | flops 101711872 | bytes 6423552 | tf_op jit(solution)/shard_map/dot_general | solution.py:89
  320.9 4.6 collective-permute-start.13
  325.6 4.2 fusion.52
  330.5 11.6 %collective-permute-done.12 = f32[16,1,64,256]{3,0,2,1:T(8,128)S(1)} collective-permute-done((f32[16,1,64,256]{3,0,2,1:T(8,128)S(1)}, f32[16,1,64,256]{3,0,2,1:T(8,128)S(1)}, u32[]{:S(2)}, u32[]{:S(2)}) %collective-permute-start.12) | collective-permute-done | bytes 1048608 | tf_op jit(solution)/shard_map/ppermute | solution.py:23
  342.1 18.0 %collective-permute-done.13 = f32[16,1,64,256]{3,0,2,1:T(8,128)S(1)} collective-permute-done((f32[16,1,64,256]{3,0,2,1:T(8,128)S(1)}, f32[16,1,64,256]{3,0,2,1:T(8,128)S(1)}, u32[]{:S(2)}, u32[]{:S(2)}) %collective-permute-start.13) | collective-permute-done | bytes 1048608 | tf_op jit(solution)/shard_map/ppermute | solution.py:21
  360.0 1.9 collective-permute-start.15
  363.3 2.7 fusion.83
  366.0 2.6 copy.101
  368.6 3.2 fusion.14
  373.1 2.9 convolution_bitcast_fusion.1
  376.0 62.5 %all-reduce.10 = (f32[16,16]{1,0:T(8,128)S(1)}, f32[16,16]{0,1:T(8,128)S(1)}) all-reduce(f32[16,16]{1,0:T(8,128)S(1)} %fusion.83, f32[16,16]{0,1:T(8,128)S(1)} %convolution_bitcast_fusion.1), channel_id=1, replica_groups=mesh['regions'=2,'gz'=8,'gy'=2] {'gz','gy'}, use_global_device_ids=true, to_apply=%region_10.13 | all-reduce | flops 512 | bytes 4096 | tf_op jit(solution)/shard_map/psum | solution.py:113
  442.9 4.5 fusion.42
  447.5 5.7 %fusion.49 = f32[16,2,64,256]{3,0,2,1:T(8,128)S(1)} fusion(f32[16,2,64,256]{3,0,2,1:T(8,128)S(1)} %fusion.42, f32[16,2,64,256]{3,0,2,1:T(8,128)S(1)} %copy-done.6, f32[16,2,64,256]{3,2,1,0:T(8,128)} %param.7, f32[2,64,256,16]{2,1,0,3:T(8,128)S(1)} %bitcast.237, f32[16,16]{1,0:T(8,128)S(1)} %fusion.124), kind=kOutput, calls=%fused_computation.76 | convolution fusion | flops 102236160 | bytes 10486784 | tf_op jit(solution)/shard_map/dot_general | solution.py:89
  453.2 2.5 copy.64
  457.0 2.9 fusion.71
  459.8 2.5 copy.65
  (101 shorter events, 42.3 us)
Async XLA Ops:
  2.5 8.4 %collective-permute-start.1 = (f32[2,1,64,256]{3,2,1,0:T(8,128)S(1)}, f32[2,1,64,256]{3,2,1,0:T(8,128)S(1)}, u32[]{:S(2)}, u32[]{:S(2)}) collective-permute-start(f32[2,1,64,256]{3,2,1,0:T(8,128)S(1)} %get-tuple-element.52), channel_id=1, source_target_pairs={{2,0},{4,2},{6,4},{8,6},{10,8},{12,10},{14,12},{3,1},{5,3},{7,5},{... | collective-permute-start | bytes 393224 | tf_op jit(solution)/shard_map/ppermute | solution.py:23
  3.8 10.0 %collective-permute-start = (f32[2,1,64,256]{3,2,1,0:T(8,128)S(1)}, f32[2,1,64,256]{3,2,1,0:T(8,128)S(1)}, u32[]{:S(2)}, u32[]{:S(2)}) collective-permute-start(f32[2,1,64,256]{3,2,1,0:T(8,128)S(1)} %get-tuple-element.51), channel_id=1, source_target_pairs={{0,2},{2,4},{4,6},{6,8},{8,10},{10,12},{12,14},{1,3},{3,5},{5,7},{... | collective-permute-start | bytes 393224 | tf_op jit(solution)/shard_map/ppermute | solution.py:21
  13.9 4.3 collective-permute-start.3
  15.2 3.8 collective-permute-start.2
  19.1 1.6 copy-start
  22.1 28.1 %collective-permute-start.4 = (f32[16,1,64,256]{3,0,2,1:T(8,128)S(1)}, f32[16,1,64,256]{3,0,2,1:T(8,128)S(1)}, u32[]{:S(2)}, u32[]{:S(2)}) collective-permute-start(f32[16,1,64,256]{3,0,2,1:T(8,128)S(1)} %get-tuple-element.36), channel_id=1, source_target_pairs={{2,0},{4,2},{6,4},{8,6},{10,8},{12,10},{14,12},{3,1},{5,3},{7,5},{... | collective-permute-start | bytes 3145736 | tf_op jit(solution)/shard_map/ppermute | solution.py:23
  23.4 49.4 %collective-permute-start.5 = (f32[16,1,64,256]{3,0,2,1:T(8,128)S(1)}, f32[16,1,64,256]{3,0,2,1:T(8,128)S(1)}, u32[]{:S(2)}, u32[]{:S(2)}) collective-permute-start(f32[16,1,64,256]{3,0,2,1:T(8,128)S(1)} %get-tuple-element.35), channel_id=1, source_target_pairs={{0,2},{2,4},{4,6},{6,8},{8,10},{10,12},{12,14},{1,3},{3,5},{5,7},{... | collective-permute-start | bytes 3145736 | tf_op jit(solution)/shard_map/ppermute | solution.py:21
  72.8 6.2 %collective-permute-start.7 = (f32[16,4,1,256]{3,0,2,1:T(8,128)S(1)}, f32[16,4,1,256]{3,0,2,1:T(8,128)S(1)}, u32[]{:S(2)}, u32[]{:S(2)}) collective-permute-start(f32[16,4,1,256]{3,0,2,1:T(8,128)S(1)} %get-tuple-element.24), channel_id=1, source_target_pairs={{0,1},{2,3},{4,5},{6,7},{8,9},{10,11},{12,13},{14,15},{16,17},{18,... | collective-permute-start | bytes 196616 | tf_op jit(solution)/shard_map/ppermute | solution.py:21
  74.7 4.3 collective-permute-start.6
  172.8 22.4 %collective-permute-start.8 = (f32[16,1,64,256]{3,0,2,1:T(8,128)S(1)}, f32[16,1,64,256]{3,0,2,1:T(8,128)S(1)}, u32[]{:S(2)}, u32[]{:S(2)}) collective-permute-start(f32[16,1,64,256]{3,0,2,1:T(8,128)S(1)} %get-tuple-element.32), channel_id=1, source_target_pairs={{2,0},{4,2},{6,4},{8,6},{10,8},{12,10},{14,12},{3,1},{5,3},{7,5},{... | collective-permute-start | bytes 3145736 | tf_op jit(solution)/shard_map/ppermute | solution.py:23
  174.1 39.1 %collective-permute-start.9 = (f32[16,1,64,256]{3,0,2,1:T(8,128)S(1)}, f32[16,1,64,256]{3,0,2,1:T(8,128)S(1)}, u32[]{:S(2)}, u32[]{:S(2)}) collective-permute-start(f32[16,1,64,256]{3,0,2,1:T(8,128)S(1)} %get-tuple-element.31), channel_id=1, source_target_pairs={{0,2},{2,4},{4,6},{6,8},{8,10},{10,12},{12,14},{1,3},{3,5},{5,7},{... | collective-permute-start | bytes 3145736 | tf_op jit(solution)/shard_map/ppermute | solution.py:21
  213.2 9.0 %collective-permute-start.11 = (f32[16,4,1,256]{3,0,2,1:T(8,128)S(1)}, f32[16,4,1,256]{3,0,2,1:T(8,128)S(1)}, u32[]{:S(2)}, u32[]{:S(2)}) collective-permute-start(f32[16,4,1,256]{3,0,2,1:T(8,128)S(1)} %get-tuple-element.22), channel_id=1, source_target_pairs={{0,1},{2,3},{4,5},{6,7},{8,9},{10,11},{12,13},{14,15},{16,17},{18,... | collective-permute-start | bytes 196616 | tf_op jit(solution)/shard_map/ppermute | solution.py:21
  215.2 7.1 %collective-permute-start.10 = (f32[16,4,1,256]{3,0,2,1:T(8,128)S(1)}, f32[16,4,1,256]{3,0,2,1:T(8,128)S(1)}, u32[]{:S(2)}, u32[]{:S(2)}) collective-permute-start(f32[16,4,1,256]{3,0,2,1:T(8,128)S(1)} %get-tuple-element.21), channel_id=1, source_target_pairs={{1,0},{3,2},{5,4},{7,6},{9,8},{11,10},{13,12},{15,14},{17,16},{19,... | collective-permute-start | bytes 196616 | tf_op jit(solution)/shard_map/ppermute | solution.py:23
  319.3 6.2 %copy-start.2 = (f32[2,8,128,256]{3,2,1,0:T(8,128)S(1)}, f32[2,8,128,256]{3,2,1,0:T(8,128)}, u32[]{:S(2)}) copy-start(f32[2,8,128,256]{3,2,1,0:T(8,128)} %copy.97) | copy-start | bytes 6291460
  319.5 22.6 %collective-permute-start.12 = (f32[16,1,64,256]{3,0,2,1:T(8,128)S(1)}, f32[16,1,64,256]{3,0,2,1:T(8,128)S(1)}, u32[]{:S(2)}, u32[]{:S(2)}) collective-permute-start(f32[16,1,64,256]{3,0,2,1:T(8,128)S(1)} %get-tuple-element.28), channel_id=1, source_target_pairs={{2,0},{4,2},{6,4},{8,6},{10,8},{12,10},{14,12},{3,1},{5,3},{7,5},{... | collective-permute-start | bytes 3145736 | tf_op jit(solution)/shard_map/ppermute | solution.py:23
  320.9 39.1 %collective-permute-start.13 = (f32[16,1,64,256]{3,0,2,1:T(8,128)S(1)}, f32[16,1,64,256]{3,0,2,1:T(8,128)S(1)}, u32[]{:S(2)}, u32[]{:S(2)}) collective-permute-start(f32[16,1,64,256]{3,0,2,1:T(8,128)S(1)} %get-tuple-element.27), channel_id=1, source_target_pairs={{0,2},{2,4},{4,6},{6,8},{8,10},{10,12},{12,14},{1,3},{3,5},{5,7},{... | collective-permute-start | bytes 3145736 | tf_op jit(solution)/shard_map/ppermute | solution.py:21
  330.5 32.8 %copy-start.1 = (f32[16,2,64,256]{3,0,2,1:T(8,128)S(1)}, f32[16,2,64,256]{3,0,2,1:T(8,128)}, u32[]{:S(2)}) copy-start(f32[16,2,64,256]{3,0,2,1:T(8,128)} %fusion.68) | copy-start | bytes 6291460
  360.0 8.5 %collective-permute-start.15 = (f32[16,4,1,256]{3,0,2,1:T(8,128)S(1)}, f32[16,4,1,256]{3,0,2,1:T(8,128)S(1)}, u32[]{:S(2)}, u32[]{:S(2)}) collective-permute-start(f32[16,4,1,256]{3,0,2,1:T(8,128)S(1)} %get-tuple-element.20), channel_id=1, source_target_pairs={{0,1},{2,3},{4,5},{6,7},{8,9},{10,11},{12,13},{14,15},{16,17},{18,... | collective-permute-start | bytes 196616 | tf_op jit(solution)/shard_map/ppermute | solution.py:21
  362.0 6.6 %collective-permute-start.14 = (f32[16,4,1,256]{3,0,2,1:T(8,128)S(1)}, f32[16,4,1,256]{3,0,2,1:T(8,128)S(1)}, u32[]{:S(2)}, u32[]{:S(2)}) collective-permute-start(f32[16,4,1,256]{3,0,2,1:T(8,128)S(1)} %get-tuple-element.19), channel_id=1, source_target_pairs={{1,0},{3,2},{5,4},{7,6},{9,8},{11,10},{13,12},{15,14},{17,16},{19,... | collective-permute-start | bytes 196616 | tf_op jit(solution)/shard_map/ppermute | solution.py:23
  371.8 1.3 copy-start.4
  442.9 4.6 copy-start.3
  442.9 4.6 copy-start.6
  453.2 2.5 copy-start.5
where the time goes:
time: 469 us; the launch traced here: 463 us
  blocking collectives  186 us (40%)
  waiting for transfers between devices  109 us (23%)
  matrix products  68.6 us (15%)
  starting transfers between devices  39.8 us (8%)
  other arithmetic  33.3 us (7%)
  local copies, waits for them, and re-layouts  24.9 us (5%)
    psum x3, blocking collectives, on_device(): lax.psum((gram(residual, scaled), gram(direction, image), gram(scaled, im...  186 us
    ppermute x8, waiting for transfers between devices, extended_2(): lax.ppermute(tail, axis, [(i, (i + 1) % count) for i in range(ends)])  62.3 us
    ppermute x8, waiting for transfers between devices, extended_2(): lax.ppermute(head, axis, [((i + 1) % count, i) for i in range(ends)])  46.3 us
    dot_general x8, matrix products, combine(): lax.dot_general(weights, flat, (((0,), (0,)), ((), ())), precision=highest)  38.9 us
    ppermute x8, starting transfers between devices, extended_2(): lax.ppermute(tail, axis, [(i, (i + 1) % count) for i in range(ends)])  28.6 us
    dot_general x9, matrix products, gram(): lax.dot_general(left_flat, right_flat, (((1,), (1,)), ((), ())), precisio...  26.8 us
    unnamed x22, local copies, waits for them, and re-layouts  21.5 us
    ppermute x8, starting transfers between devices, extended_2(): lax.ppermute(head, axis, [((i + 1) % count, i) for i in range(ends)])  11.1 us
  transfers between devices with their start and end apart: 16, of which 9 were waited for; matrix products, arithmetic and copies ran while one was open for 5% of the time, Pallas kernels for 0%

commit v1 on v0

--- a/solution.py
+++ b/solution.py
@@ -110,14 +110,19 @@
         direction_ext = direction_cells(direction)
         image = apply_operator(diagonal, offsets, direction_ext)
         weighted = inverse_diag * image
-        summed_rho, curvature, cross_gram, image_gram = lax.psum(
+
+        def tell_squares(tile_in, lane_axis, along_axis="gz"):
+            latest = lax.psum(tile_in, axis_name=lane_axis)
+            return lax.psum(latest, axis_name=along_axis)
+
+        summed_rho, curvature, cross_gram, image_gram = tell_squares(
             (
                 gram(residual, scaled),
                 gram(direction, image),
                 gram(scaled, image),
                 gram(image, weighted),
             ),
-            ("gz", "gy"),
+            "gy",
         )
         step_size = spd_solve(curvature, summed_rho)
         iterate = iterate + combine(direction, step_size)

time: 469 us -> 400 us (0.85)
  blocking collectives: 186 us -> 120 us
    psum x3 -> x6, blocking collectives: 186 us -> 120 us  [the longest x3 107 us: tell_squares(): return lax.psum(latest, axis_name=along_axis)]
  transfers between devices with their start and end apart: 16 -> 16, of which waited for: 9 -> 9; matrix products, arithmetic and copies ran while one was open for 5% -> 6% of each run, Pallas kernels for 0% -> 0%
where the time goes in v1:
time: 400 us; the launch traced here: 394 us
  blocking collectives  120 us (30%)
  waiting for transfers between devices  105 us (26%)
  matrix products  68.6 us (17%)
  starting transfers between devices  39.8 us (10%)
  other arithmetic  33.6 us (8%)
  local copies, waits for them, and re-layouts  24.9 us (6%)
    psum x3, blocking collectives, tell_squares(): return lax.psum(latest, axis_name=along_axis)  107 us
    ppermute x8, waiting for transfers between devices, extended_2(): lax.ppermute(tail, axis, [(i, (i + 1) % count) for i in range(ends)])  63.4 us
    ppermute x8, waiting for transfers between devices, extended_2(): lax.ppermute(head, axis, [((i + 1) % count, i) for i in range(ends)])  41.8 us
    dot_general x8, matrix products, combine(): lax.dot_general(weights, flat, (((0,), (0,)), ((), ())), precision=highest)  38.8 us
    ppermute x8, starting transfers between devices, extended_2(): lax.ppermute(tail, axis, [(i, (i + 1) % count) for i in range(ends)])  28.6 us
    dot_general x9, matrix products, gram(): lax.dot_general(left_flat, right_flat, (((1,), (1,)), ((), ())), precisio...  26.9 us
    unnamed x22, local copies, waits for them, and re-layouts  21.5 us
    psum x3, blocking collectives, tell_squares(): latest = lax.psum(tile_in, axis_name=lane_axis)  12.9 us
  transfers between devices with their start and end apart: 16, of which 9 were waited for; matrix products, arithmetic and copies ran while one was open for 6% of the time, Pallas kernels for 0%

profile of v1, /device:TPU:0, one launch (start us, length us, event | category | flops | bytes accessed | tf_op | source)
XLA Modules:
  0.0 393.8 jit_solution(5447394982308102620)
XLA Ops:
  3.8 5.5 %collective-permute-start = (f32[2,1,64,256]{3,2,1,0:T(8,128)S(1)}, f32[2,1,64,256]{3,2,1,0:T(8,128)S(1)}, u32[]{:S(2)}, u32[]{:S(2)}) collective-permute-start(f32[2,1,64,256]{3,2,1,0:T(8,128)S(1)} %get-tuple-element.60), channel_id=1, source_target_pairs={{0,2},{2,4},{4,6},{6,8},{8,10},{10,12},{12,14},{1,3},{3,5},{5,7},{... | collective-permute-start | bytes 393224 | tf_op jit(solution)/shard_map/ppermute | solution.py:21
  10.9 3.0 collective-permute-done
  15.2 3.0 collective-permute-start.2
  23.4 5.1 %collective-permute-start.5 = (f32[16,1,64,256]{3,0,2,1:T(8,128)S(1)}, f32[16,1,64,256]{3,0,2,1:T(8,128)S(1)}, u32[]{:S(2)}, u32[]{:S(2)}) collective-permute-start(f32[16,1,64,256]{3,0,2,1:T(8,128)S(1)} %get-tuple-element.44), channel_id=1, source_target_pairs={{0,2},{2,4},{4,6},{6,8},{8,10},{10,12},{12,14},{1,3},{3,5},{5,7},{... | collective-permute-start | bytes 3145736 | tf_op jit(solution)/shard_map/ppermute | solution.py:21
  28.5 3.5 fusion.74
  32.7 17.4 %collective-permute-done.4 = f32[16,1,64,256]{3,0,2,1:T(8,128)S(1)} collective-permute-done((f32[16,1,64,256]{3,0,2,1:T(8,128)S(1)}, f32[16,1,64,256]{3,0,2,1:T(8,128)S(1)}, u32[]{:S(2)}, u32[]{:S(2)}) %collective-permute-start.4) | collective-permute-done | bytes 1048608 | tf_op jit(solution)/shard_map/ppermute | solution.py:23
  50.1 22.6 %collective-permute-done.5 = f32[16,1,64,256]{3,0,2,1:T(8,128)S(1)} collective-permute-done((f32[16,1,64,256]{3,0,2,1:T(8,128)S(1)}, f32[16,1,64,256]{3,0,2,1:T(8,128)S(1)}, u32[]{:S(2)}, u32[]{:S(2)}) %collective-permute-start.5) | collective-permute-done | bytes 1048608 | tf_op jit(solution)/shard_map/ppermute | solution.py:21
  72.8 1.9 collective-permute-start.7
  76.4 2.5 copy.93
  79.0 3.2 fusion.34
  82.2 3.8 convolution_bitcast_fusion.5
  86.0 2.7 fusion.86
  88.8 2.6 copy.95
  91.3 4.4 %all-reduce.15 = (f32[16,16]{0,1:T(8,128)S(1)}, f32[16,16]{0,1:T(8,128)S(1)}, f32[16,16]{1,0:T(8,128)S(1)}) all-reduce(f32[16,16]{0,1:T(8,128)S(1)} %fusion.74, f32[16,16]{0,1:T(8,128)S(1)} %convolution_bitcast_fusion.5, f32[16,16]{1,0:T(8,128)S(1)} %fusion.86), channel_id=1, replica_groups=mesh['regions'=2,'gz'=8,'gy'=2] {'gy'}, use_global_device_ids=true, to_apply=%region_4.6 | all-reduce | flops 768 | bytes 6144 | tf_op jit(solution)/shard_map/psum | solution.py:115
  95.7 36.0 %all-reduce.12 = (f32[16,16]{0,1:T(8,128)S(1)}, f32[16,16]{0,1:T(8,128)S(1)}, f32[16,16]{1,0:T(8,128)S(1)}) all-reduce(f32[16,16]{0,1:T(8,128)S(1)} %get-tuple-element.23, f32[16,16]{0,1:T(8,128)S(1)} %get-tuple-element.24, f32[16,16]{1,0:T(8,128)S(1)} %get-tuple-element.25), channel_id=1, replica_groups=mesh['regions'=2,'gz'=8,'gy'=2] {'gz'}, use_global_device_ids=true, to_apply=%region_5.7 | all-reduce | flops 768 | bytes 6144 | tf_op jit(solution)/shard_map/psum | solution.py:116
  136.5 6.3 %copy_subtract_fusion = f32[16,2,64,256]{3,0,2,1:T(8,128)S(1)} fusion(f32[16,2,64,256]{3,2,1,0:T(8,128)} %param.8, f32[2,64,256,16]{2,1,0,3:T(8,128)} %bitcast.241, f32[16,16]{1,0:T(8,128)S(1)} %fusion.124), kind=kOutput, calls=%fused_computation.85 | convolution fusion | flops 101187584 | bytes 6292480 | tf_op jit(solution)/shard_map/dot_general | solution.py:89
  147.6 4.5 %multiply_add_fusion.1 = f32[16,2,64,256]{3,0,2,1:T(8,128)S(1)} fusion(f32[16,2,64,256]{3,0,2,1:T(8,128)S(1)} %copy_subtract_fusion, f32[16,16,1,1]{0,1,3,2:T(8,128)S(1)} %convolution_bitcast_fusion.4, f32[2,64,256,16]{2,1,0,3:T(8,128)} %bitcast.236, f32[2,64,256]{2,1,0:T(8,128)S(1)} %get-tuple-element.26), kind=kOutput, calls=%fused_computation.11 | convolution fusion | flops 101711872 | bytes 6423552 | tf_op jit(solution)/shard_map/dot_general | solution.py:89
  153.6 4.6 %collective-permute-start.9 = (f32[16,1,64,256]{3,0,2,1:T(8,128)S(1)}, f32[16,1,64,256]{3,0,2,1:T(8,128)S(1)}, u32[]{:S(2)}, u32[]{:S(2)}) collective-permute-start(f32[16,1,64,256]{3,0,2,1:T(8,128)S(1)} %get-tuple-element.40), channel_id=1, source_target_pairs={{0,2},{2,4},{4,6},{6,8},{8,10},{10,12},{12,14},{1,3},{3,5},{5,7},{... | collective-permute-start | bytes 3145736 | tf_op jit(solution)/shard_map/ppermute | solution.py:21
  159.0 13.8 %collective-permute-done.8 = f32[16,1,64,256]{3,0,2,1:T(8,128)S(1)} collective-permute-done((f32[16,1,64,256]{3,0,2,1:T(8,128)S(1)}, f32[16,1,64,256]{3,0,2,1:T(8,128)S(1)}, u32[]{:S(2)}, u32[]{:S(2)}) %collective-permute-start.8) | collective-permute-done | bytes 1048608 | tf_op jit(solution)/shard_map/ppermute | solution.py:23
  172.8 18.2 %collective-permute-done.9 = f32[16,1,64,256]{3,0,2,1:T(8,128)S(1)} collective-permute-done((f32[16,1,64,256]{3,0,2,1:T(8,128)S(1)}, f32[16,1,64,256]{3,0,2,1:T(8,128)S(1)}, u32[]{:S(2)}, u32[]{:S(2)}) %collective-permute-start.9) | collective-permute-done | bytes 1048608 | tf_op jit(solution)/shard_map/ppermute | solution.py:21
  191.0 1.9 collective-permute-start.11
  194.8 2.8 fusion.77
  197.6 2.6 copy.97
  200.2 3.2 fusion.24
  203.4 2.9 convolution_bitcast_fusion.3
  206.3 2.8 fusion.89
  209.1 2.8 fusion.80
  211.9 2.6 copy.99
  214.4 4.4 %all-reduce.14 = (f32[16,16]{0,1:T(8,128)S(1)}, f32[16,16]{0,1:T(8,128)S(1)}, f32[16,16]{1,0:T(8,128)S(1)}, f32[16,16]{1,0:T(8,128)S(1)}) all-reduce(f32[16,16]{0,1:T(8,128)S(1)} %fusion.77, f32[16,16]{0,1:T(8,128)S(1)} %convolution_bitcast_fusion.3, f32[16,16]{1,0:T(8,128)S(1)} %fusion.89, ...), channel_id=1, replica_groups=mesh['regions'=2,'gz'=8,'gy'=2] {'gy'}, use_global_device_ids=true, to_apply=%region_10.13 | all-reduce | flops 1024 | bytes 8192 | tf_op jit(solution)/shard_map/psum | solution.py:115
  218.8 35.7 %all-reduce.11 = (f32[16,16]{0,1:T(8,128)S(1)}, f32[16,16]{0,1:T(8,128)S(1)}, f32[16,16]{1,0:T(8,128)S(1)}, f32[16,16]{1,0:T(8,128)S(1)}) all-reduce(f32[16,16]{0,1:T(8,128)S(1)} %get-tuple-element.19, f32[16,16]{0,1:T(8,128)S(1)} %get-tuple-element.20, ...), channel_id=1, replica_groups=mesh['regions'=2,'gz'=8,'gy'=2] {'gz'}, use_global_device_ids=true, to_apply=%region_11.14 | all-reduce | flops 1024 | bytes 8192 | tf_op jit(solution)/shard_map/psum | solution.py:116
  259.0 5.6 %fusion.68 = f32[16,2,64,256]{3,0,2,1:T(8,128)} fusion(f32[16,2,64,256]{3,0,2,1:T(8,128)S(1)} %copy_subtract_fusion, f32[2,64,256,16]{2,1,0,3:T(8,128)} %bitcast.240, f32[16,16]{1,0:T(8,128)S(1)} %fusion.113), kind=kOutput, calls=%fused_computation.89 | convolution fusion | flops 101187584 | bytes 6292480 | tf_op jit(solution)/shard_map/dot_general | solution.py:89
  269.6 5.2 %multiply_add_fusion = f32[16,2,64,256]{3,0,2,1:T(8,128)S(1)} fusion(f32[16,2,64,256]{3,0,2,1:T(8,128)} %fusion.68, f32[16,16,1,1]{0,1,3,2:T(8,128)S(1)} %convolution_bitcast_fusion.2, f32[2,64,256,16]{2,1,0,3:T(8,128)} %bitcast.234, f32[2,64,256]{2,1,0:T(8,128)S(1)} %get-tuple-element.26), kind=kOutput, calls=%fused_computation.6 | convolution fusion | flops 101711872 | bytes 6423552 | tf_op jit(solution)/shard_map/dot_general | solution.py:89
  276.4 4.6 %collective-permute-start.13 = (f32[16,1,64,256]{3,0,2,1:T(8,128)S(1)}, f32[16,1,64,256]{3,0,2,1:T(8,128)S(1)}, u32[]{:S(2)}, u32[]{:S(2)}) collective-permute-start(f32[16,1,64,256]{3,0,2,1:T(8,128)S(1)} %get-tuple-element.36), channel_id=1, source_target_pairs={{0,2},{2,4},{4,6},{6,8},{8,10},{10,12},{12,14},{1,3},{3,5},{5,7},{... | collective-permute-start | bytes 3145736 | tf_op jit(solution)/shard_map/ppermute | solution.py:21
  281.0 4.2 %fusion.52 = f32[16,2,64,256]{3,0,2,1:T(8,128)} fusion(f32[2,64,256,16]{2,1,0,3:T(8,128)S(1)} %bitcast.235, f32[16,16]{1,0:T(8,128)S(1)} %fusion.113), kind=kOutput, calls=%fused_computation.79 | convolution fusion | flops 100663296 | bytes 4195328 | tf_op jit(solution)/shard_map/dot_general | solution.py:89
  286.0 9.0 %collective-permute-done.12 = f32[16,1,64,256]{3,0,2,1:T(8,128)S(1)} collective-permute-done((f32[16,1,64,256]{3,0,2,1:T(8,128)S(1)}, f32[16,1,64,256]{3,0,2,1:T(8,128)S(1)}, u32[]{:S(2)}, u32[]{:S(2)}) %collective-permute-start.12) | collective-permute-done | bytes 1048608 | tf_op jit(solution)/shard_map/ppermute | solution.py:23
  295.0 18.8 %collective-permute-done.13 = f32[16,1,64,256]{3,0,2,1:T(8,128)S(1)} collective-permute-done((f32[16,1,64,256]{3,0,2,1:T(8,128)S(1)}, f32[16,1,64,256]{3,0,2,1:T(8,128)S(1)}, u32[]{:S(2)}, u32[]{:S(2)}) %collective-permute-start.13) | collective-permute-done | bytes 1048608 | tf_op jit(solution)/shard_map/ppermute | solution.py:21
  313.8 1.9 collective-permute-start.15
  317.0 2.8 fusion.83
  319.8 2.6 copy.101
  322.4 3.2 fusion.14
  326.9 2.9 convolution_bitcast_fusion.1
  329.8 4.2 %all-reduce.13 = (f32[16,16]{1,0:T(8,128)S(1)}, f32[16,16]{0,1:T(8,128)S(1)}) all-reduce(f32[16,16]{1,0:T(8,128)S(1)} %fusion.83, f32[16,16]{0,1:T(8,128)S(1)} %convolution_bitcast_fusion.1), channel_id=1, replica_groups=mesh['regions'=2,'gz'=8,'gy'=2] {'gy'}, use_global_device_ids=true, to_apply=%region_18.21 | all-reduce | flops 512 | bytes 4096 | tf_op jit(solution)/shard_map/psum | solution.py:115
  334.0 35.5 %all-reduce.10 = (f32[16,16]{1,0:T(8,128)S(1)}, f32[16,16]{0,1:T(8,128)S(1)}) all-reduce(f32[16,16]{1,0:T(8,128)S(1)} %get-tuple-element.17, f32[16,16]{0,1:T(8,128)S(1)} %get-tuple-element.18), channel_id=1, replica_groups=mesh['regions'=2,'gz'=8,'gy'=2] {'gz'}, use_global_device_ids=true, to_apply=%region_19.22 | all-reduce | flops 512 | bytes 4096 | tf_op jit(solution)/shard_map/psum | solution.py:116
  374.0 4.5 %fusion.42 = f32[16,2,64,256]{3,0,2,1:T(8,128)S(1)} fusion(f32[16,16,1,1]{0,1,3,2:T(8,128)S(1)} %convolution_bitcast_fusion, f32[2,64,256,16]{2,1,0,3:T(8,128)} %bitcast.239), kind=kOutput, calls=%fused_computation.68 | convolution fusion | flops 100663296 | bytes 4195328 | tf_op jit(solution)/shard_map/dot_general | solution.py:89
  378.6 5.7 %fusion.49 = f32[16,2,64,256]{3,0,2,1:T(8,128)S(1)} fusion(f32[16,2,64,256]{3,0,2,1:T(8,128)S(1)} %fusion.42, f32[16,2,64,256]{3,0,2,1:T(8,128)S(1)} %copy-done.6, f32[16,2,64,256]{3,2,1,0:T(8,128)} %param.7, f32[2,64,256,16]{2,1,0,3:T(8,128)S(1)} %bitcast.237, f32[16,16]{1,0:T(8,128)S(1)} %fusion.124), kind=kOutput, calls=%fused_computation.76 | convolution fusion | flops 102236160 | bytes 10486784 | tf_op jit(solution)/shard_map/dot_general | solution.py:89
  384.3 2.5 copy.64
  388.0 2.9 fusion.71
  390.9 2.5 copy.65
  (104 shorter events, 47.4 us)
Async XLA Ops:
  2.5 8.4 %collective-permute-start.1 = (f32[2,1,64,256]{3,2,1,0:T(8,128)S(1)}, f32[2,1,64,256]{3,2,1,0:T(8,128)S(1)}, u32[]{:S(2)}, u32[]{:S(2)}) collective-permute-start(f32[2,1,64,256]{3,2,1,0:T(8,128)S(1)} %get-tuple-element.61), channel_id=1, source_target_pairs={{2,0},{4,2},{6,4},{8,6},{10,8},{12,10},{14,12},{3,1},{5,3},{7,5},{... | collective-permute-start | bytes 393224 | tf_op jit(solution)/shard_map/ppermute | solution.py:23
  3.8 10.0 %collective-permute-start = (f32[2,1,64,256]{3,2,1,0:T(8,128)S(1)}, f32[2,1,64,256]{3,2,1,0:T(8,128)S(1)}, u32[]{:S(2)}, u32[]{:S(2)}) collective-permute-start(f32[2,1,64,256]{3,2,1,0:T(8,128)S(1)} %get-tuple-element.60), channel_id=1, source_target_pairs={{0,2},{2,4},{4,6},{6,8},{8,10},{10,12},{12,14},{1,3},{3,5},{5,7},{... | collective-permute-start | bytes 393224 | tf_op jit(solution)/shard_map/ppermute | solution.py:21
  13.9 4.3 %collective-permute-start.3 = (f32[2,4,1,256]{3,2,1,0:T(1,128)S(1)}, f32[2,4,1,256]{3,2,1,0:T(1,128)S(1)}, u32[]{:S(2)}, u32[]{:S(2)}) collective-permute-start(f32[2,4,1,256]{3,2,1,0:T(1,128)S(1)} %get-tuple-element.55), channel_id=1, source_target_pairs={{1,0},{3,2},{5,4},{7,6},{9,8},{11,10},{13,12},{15,14},{17,16},{19,... | collective-permute-start | bytes 24584 | tf_op jit(solution)/shard_map/ppermute | solution.py:23
  15.2 3.8 collective-permute-start.2
  19.1 1.6 copy-start
  22.1 28.1 %collective-permute-start.4 = (f32[16,1,64,256]{3,0,2,1:T(8,128)S(1)}, f32[16,1,64,256]{3,0,2,1:T(8,128)S(1)}, u32[]{:S(2)}, u32[]{:S(2)}) collective-permute-start(f32[16,1,64,256]{3,0,2,1:T(8,128)S(1)} %get-tuple-element.45), channel_id=1, source_target_pairs={{2,0},{4,2},{6,4},{8,6},{10,8},{12,10},{14,12},{3,1},{5,3},{7,5},{... | collective-permute-start | bytes 3145736 | tf_op jit(solution)/shard_map/ppermute | solution.py:23
  23.4 49.4 %collective-permute-start.5 = (f32[16,1,64,256]{3,0,2,1:T(8,128)S(1)}, f32[16,1,64,256]{3,0,2,1:T(8,128)S(1)}, u32[]{:S(2)}, u32[]{:S(2)}) collective-permute-start(f32[16,1,64,256]{3,0,2,1:T(8,128)S(1)} %get-tuple-element.44), channel_id=1, source_target_pairs={{0,2},{2,4},{4,6},{6,8},{8,10},{10,12},{12,14},{1,3},{3,5},{5,7},{... | collective-permute-start | bytes 3145736 | tf_op jit(solution)/shard_map/ppermute | solution.py:21
  72.8 6.2 %collective-permute-start.7 = (f32[16,4,1,256]{3,0,2,1:T(8,128)S(1)}, f32[16,4,1,256]{3,0,2,1:T(8,128)S(1)}, u32[]{:S(2)}, u32[]{:S(2)}) collective-permute-start(f32[16,4,1,256]{3,0,2,1:T(8,128)S(1)} %get-tuple-element.33), channel_id=1, source_target_pairs={{0,1},{2,3},{4,5},{6,7},{8,9},{10,11},{12,13},{14,15},{16,17},{18,... | collective-permute-start | bytes 196616 | tf_op jit(solution)/shard_map/ppermute | solution.py:21
  74.7 4.3 %collective-permute-start.6 = (f32[16,4,1,256]{3,0,2,1:T(8,128)S(1)}, f32[16,4,1,256]{3,0,2,1:T(8,128)S(1)}, u32[]{:S(2)}, u32[]{:S(2)}) collective-permute-start(f32[16,4,1,256]{3,0,2,1:T(8,128)S(1)} %get-tuple-element.32), channel_id=1, source_target_pairs={{1,0},{3,2},{5,4},{7,6},{9,8},{11,10},{13,12},{15,14},{17,16},{19,... | collective-permute-start | bytes 196616 | tf_op jit(solution)/shard_map/ppermute | solution.py:23
  152.3 20.5 %collective-permute-start.8 = (f32[16,1,64,256]{3,0,2,1:T(8,128)S(1)}, f32[16,1,64,256]{3,0,2,1:T(8,128)S(1)}, u32[]{:S(2)}, u32[]{:S(2)}) collective-permute-start(f32[16,1,64,256]{3,0,2,1:T(8,128)S(1)} %get-tuple-element.41), channel_id=1, source_target_pairs={{2,0},{4,2},{6,4},{8,6},{10,8},{12,10},{14,12},{3,1},{5,3},{7,5},{... | collective-permute-start | bytes 3145736 | tf_op jit(solution)/shard_map/ppermute | solution.py:23
  153.6 37.4 %collective-permute-start.9 = (f32[16,1,64,256]{3,0,2,1:T(8,128)S(1)}, f32[16,1,64,256]{3,0,2,1:T(8,128)S(1)}, u32[]{:S(2)}, u32[]{:S(2)}) collective-permute-start(f32[16,1,64,256]{3,0,2,1:T(8,128)S(1)} %get-tuple-element.40), channel_id=1, source_target_pairs={{0,2},{2,4},{4,6},{6,8},{8,10},{10,12},{12,14},{1,3},{3,5},{5,7},{... | collective-permute-start | bytes 3145736 | tf_op jit(solution)/shard_map/ppermute | solution.py:21
  191.0 9.1 %collective-permute-start.11 = (f32[16,4,1,256]{3,0,2,1:T(8,128)S(1)}, f32[16,4,1,256]{3,0,2,1:T(8,128)S(1)}, u32[]{:S(2)}, u32[]{:S(2)}) collective-permute-start(f32[16,4,1,256]{3,0,2,1:T(8,128)S(1)} %get-tuple-element.31), channel_id=1, source_target_pairs={{0,1},{2,3},{4,5},{6,7},{8,9},{10,11},{12,13},{14,15},{16,17},{18,... | collective-permute-start | bytes 196616 | tf_op jit(solution)/shard_map/ppermute | solution.py:21
  193.0 7.2 %collective-permute-start.10 = (f32[16,4,1,256]{3,0,2,1:T(8,128)S(1)}, f32[16,4,1,256]{3,0,2,1:T(8,128)S(1)}, u32[]{:S(2)}, u32[]{:S(2)}) collective-permute-start(f32[16,4,1,256]{3,0,2,1:T(8,128)S(1)} %get-tuple-element.30), channel_id=1, source_target_pairs={{1,0},{3,2},{5,4},{7,6},{9,8},{11,10},{13,12},{15,14},{17,16},{19,... | collective-permute-start | bytes 196616 | tf_op jit(solution)/shard_map/ppermute | solution.py:23
  274.8 6.2 %copy-start.2 = (f32[2,8,128,256]{3,2,1,0:T(8,128)S(1)}, f32[2,8,128,256]{3,2,1,0:T(8,128)}, u32[]{:S(2)}) copy-start(f32[2,8,128,256]{3,2,1,0:T(8,128)} %copy.97) | copy-start | bytes 6291460
  275.0 20.0 %collective-permute-start.12 = (f32[16,1,64,256]{3,0,2,1:T(8,128)S(1)}, f32[16,1,64,256]{3,0,2,1:T(8,128)S(1)}, u32[]{:S(2)}, u32[]{:S(2)}) collective-permute-start(f32[16,1,64,256]{3,0,2,1:T(8,128)S(1)} %get-tuple-element.37), channel_id=1, source_target_pairs={{2,0},{4,2},{6,4},{8,6},{10,8},{12,10},{14,12},{3,1},{5,3},{7,5},{... | collective-permute-start | bytes 3145736 | tf_op jit(solution)/shard_map/ppermute | solution.py:23
  276.4 37.4 %collective-permute-start.13 = (f32[16,1,64,256]{3,0,2,1:T(8,128)S(1)}, f32[16,1,64,256]{3,0,2,1:T(8,128)S(1)}, u32[]{:S(2)}, u32[]{:S(2)}) collective-permute-start(f32[16,1,64,256]{3,0,2,1:T(8,128)S(1)} %get-tuple-element.36), channel_id=1, source_target_pairs={{0,2},{2,4},{4,6},{6,8},{8,10},{10,12},{12,14},{1,3},{3,5},{5,7},{... | collective-permute-start | bytes 3145736 | tf_op jit(solution)/shard_map/ppermute | solution.py:21
  286.0 31.0 %copy-start.1 = (f32[16,2,64,256]{3,0,2,1:T(8,128)S(1)}, f32[16,2,64,256]{3,0,2,1:T(8,128)}, u32[]{:S(2)}) copy-start(f32[16,2,64,256]{3,0,2,1:T(8,128)} %fusion.68) | copy-start | bytes 6291460
  313.8 8.6 %collective-permute-start.15 = (f32[16,4,1,256]{3,0,2,1:T(8,128)S(1)}, f32[16,4,1,256]{3,0,2,1:T(8,128)S(1)}, u32[]{:S(2)}, u32[]{:S(2)}) collective-permute-start(f32[16,4,1,256]{3,0,2,1:T(8,128)S(1)} %get-tuple-element.29), channel_id=1, source_target_pairs={{0,1},{2,3},{4,5},{6,7},{8,9},{10,11},{12,13},{14,15},{16,17},{18,... | collective-permute-start | bytes 196616 | tf_op jit(solution)/shard_map/ppermute | solution.py:21
  315.7 6.6 %collective-permute-start.14 = (f32[16,4,1,256]{3,0,2,1:T(8,128)S(1)}, f32[16,4,1,256]{3,0,2,1:T(8,128)S(1)}, u32[]{:S(2)}, u32[]{:S(2)}) collective-permute-start(f32[16,4,1,256]{3,0,2,1:T(8,128)S(1)} %get-tuple-element.28), channel_id=1, source_target_pairs={{1,0},{3,2},{5,4},{7,6},{9,8},{11,10},{13,12},{15,14},{17,16},{19,... | collective-permute-start | bytes 196616 | tf_op jit(solution)/shard_map/ppermute | solution.py:23
  325.6 1.3 copy-start.4
  374.0 4.6 %copy-start.3 = (f32[2,8,128,256]{3,2,1,0:T(8,128)S(1)}, f32[2,8,128,256]{3,2,1,0:T(8,128)}, u32[]{:S(2)}) copy-start(f32[2,8,128,256]{3,2,1,0:T(8,128)} %copy.93) | copy-start | bytes 6291460
  374.0 4.6 %copy-start.6 = (f32[16,2,64,256]{3,0,2,1:T(8,128)S(1)}, f32[16,2,64,256]{3,0,2,1:T(8,128)}, u32[]{:S(2)}) copy-start(f32[16,2,64,256]{3,0,2,1:T(8,128)} %fusion.52) | copy-start | bytes 6291460
  384.3 2.5 copy-start.5
